TPU v7x, 32 devices: a whole 2x2x4 slice. The times are simulated.
32 devices in a mesh: py: 4 (over y, x), px: 8 (over z, core).
Axes of the slice: x: 2, y: 2, z: 4, core: 2. Of those that a mesh axis runs over, the one named last changes fastest.
Arguments:
- movie: bfloat16 [256, 128, 2048], P('py', 'px'), may hold values from -6 to 6
- traces: bfloat16 [4096, 2048], P('py', 'px'), may hold values from -0.125 to 0.125
- footprints: float32 [256, 128, 512], P('py', 'px'), may hold values from 0 to 1
- block_ids: int32 [4, 8, 4], P('py', 'px'), may hold values from 0 to 32, as said below
Outputs:
- updated: float32 [256, 128, 512], P('py', 'px')
Inputs may be any that keep to these rules, and one draw needn't show every extreme that they name: `block_ids`: in each tile's list of 4 entries the live entries come first and are distinct block numbers below 32; the remaining entries equal 32 and mark empty slots. Every tile has at least one live entry, and some tile has all 4 live.
All inputs are finite; a program needn't handle non-finite values.
Results may differ from a plain program's by a relative error of at most 0.0003.
Values may be sent and summed in bfloat16 or wider, within the bound.
A program may use at most 64 MiB of HBM per device.

v0:
```python
import jax
import jax.numpy as jnp
from jax import lax
from jax.sharding import PartitionSpec as P

K = 4096
BLK = 128
SLOTS = 4
ITERS = 2


def accumulate(tile_movie, picked):
    cross = lax.dot_general(
        tile_movie, picked, (((1,), (1,)), ((), ())), preferred_element_type=jnp.float32
    )
    gram = lax.dot_general(
        picked, picked, (((1,), (1,)), ((), ())), preferred_element_type=jnp.float32
    )
    return (cross, gram)


def per_device(movie, traces, footprints, block_ids):
    rows, cols, frames = movie.shape
    pixels = rows * cols
    width = SLOTS * BLK
    nblk = K // BLK
    tile_movie = movie.reshape(pixels, frames)
    ids = block_ids.reshape(SLOTS)
    onehot = (ids[:, None] == jnp.arange(nblk, dtype=jnp.int32)[None, :]).astype(jnp.float32)
    live = jnp.sum(onehot, axis=1)
    span_all = lax.all_gather(traces, "py", axis=0, tiled=True)
    span_len = span_all.shape[1]
    row_ids = lax.all_gather(block_ids, "px", axis=1, tiled=True).reshape(-1, SLOTS)
    route = (row_ids[:, :, None] == jnp.arange(nblk, dtype=jnp.int32)[None, None, :]).astype(
        jnp.bfloat16
    )
    outgoing = jnp.einsum(
        "rsb,bnw->rsnw",
        route,
        span_all.reshape(nblk, BLK, span_len),
        preferred_element_type=jnp.float32,
    )
    outgoing = outgoing.astype(jnp.bfloat16).reshape(row_ids.shape[0], width, span_len)
    received = lax.all_to_all(outgoing, "px", split_axis=0, concat_axis=2, tiled=True)
    mine = received.reshape(width, frames)
    cross, gram = accumulate(tile_movie, mine)
    column_live = jnp.repeat(live, BLK)
    denom = jnp.diagonal(gram) + 1e-06 + (1.0 - column_live)
    current = footprints.reshape(pixels, width) * column_live[None, :]
    pixall = pixels * lax.axis_size("py") * lax.axis_size("px")
    for step in range(ITERS):
        for slot in range(SLOTS):
            low = slot * BLK
            resid = cross[:, low : low + BLK] - jnp.dot(
                current, gram[:, low : low + BLK], precision=lax.Precision.HIGHEST
            )
            fresh = jnp.maximum(
                current[:, low : low + BLK] + resid / denom[None, low : low + BLK], 0.0
            )
            current = current.at[:, low : low + BLK].set(fresh)
        colsq = jnp.sum(current * current, axis=0).reshape(SLOTS, BLK)
        partial_value = jnp.einsum("sb,sn->bn", onehot, colsq, precision=lax.Precision.HIGHEST)
        totals = lax.psum(partial_value, ("py", "px"))
        factor = 1.0 / jnp.sqrt(totals / pixall + 1e-06)
        scale = jnp.einsum("sb,bn->sn", onehot, factor, precision=lax.Precision.HIGHEST).reshape(
            width
        )
        current = current * scale[None, :]
    return current.reshape(rows, cols, width)


def solution(mesh):
    return jax.shard_map(
        per_device,
        mesh=mesh,
        in_specs=(P("py", "px", None), P("py", "px"), P("py", "px", None), P("py", "px", None)),
        out_specs=P("py", "px", None),
        check_vma=False,
    )
```

profile of v0, /device:TPU:0, one launch (start us, length us, event | category | flops | bytes accessed | tf_op | source)
XLA Modules:
  0.0 233.0 jit_solution(12457084238456742489)
XLA Ops:
  7.3 13.6 %all_gather.6 = s32[1,8,4]{2,0,1:T(1,128)S(1)} all-gather(s32[1,1,4]{2,0,1:T(1,128)} %bitcast.62), channel_id=1, replica_groups=mesh['py'=4,'px'=8] {'px'}, dimensions={1}, use_global_device_ids=true | all-gather | bytes 144 | tf_op jit(solution)/shard_map/all_gather | solution.py:33
  21.0 26.1 %all-gather.2.cloned.1.call-done = bf16[4096,256]{1,0:T(8,128)(2,1)} async-done(((bf16[1024,256]{1,0:T(8,128)(2,1)}), bf16[4096,256]{1,0:T(8,128)(2,1)}) %all-gather.2.cloned.1.call-update) | async-done | bytes 2097168 | tf_op jit(solution)/shard_map/all_gather | solution.py:31
  47.1 2.9 %fusion.5 = bf16[8,4,128,256]{3,0,2,1:T(8,128)(2,1)S(1)} fusion(bf16[32,128,256]{2,1,0:T(8,128)(2,1)} %bitcast.60, s32[8,4]{0,1:T(4,128)S(1)} %bitcast.61), kind=kOutput, calls=%fused_computation.8 | convolution fusion | flops 68158464 | bytes 4194432 | tf_op jit(solution)/shard_map/rsb,bnw->rsnw/dot_general | solution.py:37
  50.0 1.7 copy.50
  51.8 4.7 %all-to-all-start = ((bf16[8,512,256]{2,1,0:T(8,128)(2,1)}), bf16[8,512,256]{2,1,0:T(8,128)(2,1)}, u32[]{:S(2)}, u32[]{:S(2)}) async-start(bf16[8,512,256]{2,1,0:T(8,128)(2,1)} %copy.50), calls=%async_computation | async-start | bytes 4194304 | tf_op jit(solution)/shard_map/all_to_all | solution.py:44
  56.5 1.8 copy.46
  60.0 1.8 broadcast_multiply_fusion.2
  61.8 43.9 %all-to-all-done = bf16[8,512,256]{2,1,0:T(8,128)(2,1)} async-done(((bf16[8,512,256]{2,1,0:T(8,128)(2,1)}), bf16[8,512,256]{2,1,0:T(8,128)(2,1)}, u32[]{:S(2)}, u32[]{:S(2)}) %all-to-all-start) | async-done | bytes 2097184 | tf_op jit(solution)/shard_map/all_to_all | solution.py:44
  105.6 3.5 %fusion.8 = f32[512,512]{1,0:T(8,128)S(1)} fusion(bf16[8,512,256]{2,1,0:T(8,128)(2,1)} %all-to-all-done), kind=kOutput, calls=%fused_computation.10 | convolution fusion | flops 1073741824 | bytes 3145728 | tf_op jit(solution)/shard_map/dot_general | solution.py:16
  109.1 4.5 %gather_fusion = f32[512]{0:T(512)S(1)} fusion(f32[512,512]{1,0:T(8,128)S(1)} %fusion.8, s32[512]{0:T(512)S(1)} %bitcast.56), kind=kCustom, calls=%fused_computation | custom fusion | bytes 8192 | tf_op jit(solution)/shard_map/jit(diagonal)/cond/branch_0_fun/gather | solution.py:48
  113.7 3.9 %copy.51 = bf16[1,512,8,256]{1,3,2,0:T(8,128)(2,1)} copy(bf16[1,512,8,256]{3,1,2,0:T(8,128)(2,1)} %bitcast.11) | data formatting | bytes 4194304 | tf_op jit(solution)/shard_map/all_to_all | solution.py:44
  117.7 5.2 %convolution_bitcast_fusion = f32[1024,512]{0,1:T(8,128)S(1)} fusion(bf16[512,2048]{0,1:T(8,128)(2,1)} %bitcast.59, bf16[1024,2048]{1,0:T(8,128)(2,1)} %bitcast.68), kind=kOutput, calls=%fused_computation.9 | convolution fusion | flops 2147483648 | bytes 8388608 | tf_op jit(solution)/shard_map/dot_general | solution.py:13
  122.9 2.1 fusion.40
  125.0 2.2 fusion.36
  127.2 2.1 fusion.32
  129.4 1.5 fusion.28
  131.3 37.2 %psum.14 = f32[32,128]{1,0:T(8,128)S(1)} all-reduce(f32[32,128]{1,0:T(8,128)S(1)} %fusion.64), channel_id=1, replica_groups=mesh['py'=4,'px'=8] {'py','px'}, use_global_device_ids=true, to_apply=%region_5.6 | all-reduce | flops 4096 | bytes 32768 | tf_op jit(solution)/shard_map/psum | solution.py:63
  170.3 2.1 fusion.25
  172.4 2.1 fusion.21
  174.6 2.0 fusion.17
  176.7 1.4 fusion.13
  179.9 42.4 %psum.15 = f32[32,128]{1,0:T(8,128)S(1)} all-reduce(f32[32,128]{1,0:T(8,128)S(1)} %fusion.62), channel_id=1, replica_groups=mesh['py'=4,'px'=8] {'py','px'}, use_global_device_ids=true, to_apply=%region_7.8 | all-reduce | flops 4096 | bytes 32768 | tf_op jit(solution)/shard_map/psum | solution.py:63
  222.5 1.8 broadcast_multiply_fusion
  224.3 1.8 copy.60
  (35 shorter events, 7.0 us)
Async XLA Ops:
  6.5 40.6 %all-gather.2.cloned.1.call-start = ((), (), s32[]{:S(2)}) async-start(), calls=%async_computation.1 | async-start | bytes 2621440 | tf_op jit(solution)/shard_map/all_gather | solution.py:31
  51.7 4.7 %copy-start.3 = (f32[64,16,512]{2,1,0:T(8,128)S(1)}, f32[64,16,512]{2,1,0:T(8,128)}, u32[]{:S(2)}) copy-start(f32[64,16,512]{2,1,0:T(8,128)} %param.22) | copy-start | bytes 6291460
  51.8 53.9 %all-to-all-start = ((bf16[8,512,256]{2,1,0:T(8,128)(2,1)}), bf16[8,512,256]{2,1,0:T(8,128)(2,1)}, u32[]{:S(2)}, u32[]{:S(2)}) async-start(bf16[8,512,256]{2,1,0:T(8,128)(2,1)} %copy.50), calls=%async_computation | async-start | bytes 4194304 | tf_op jit(solution)/shard_map/all_to_all | solution.py:44
  56.5 3.2 %copy-start.4 = (s32[1,1,4]{2,1,0:T(1,128)S(1)}, s32[1,1,4]{2,1,0:T(1,128)}, u32[]{:S(2)}) copy-start(s32[1,1,4]{2,1,0:T(1,128)} %param.23) | copy-start | bytes 52
  122.9 6.5 %copy-start.1 = (f32[1024,512]{0,1:T(8,128)}, f32[1024,512]{0,1:T(8,128)S(1)}, u32[]{:S(2)}) copy-start(f32[1024,512]{0,1:T(8,128)S(1)} %convolution_bitcast_fusion) | copy-start | bytes 6291460
  168.7 1.6 copy-start.2
  178.1 1.3 copy-start
Sparse Core Ops, SparseCore 0:
  9.2 37.8 all-gather.1
where the time goes:
time: 234 us; the launch traced here: 233 us
  blocking collectives  93.2 us (40%)
  waiting for transfers between devices  70.7 us (30%)
  matrix products  27.9 us (12%)
  local copies, waits for them, and re-layouts  17 us (7%)
  between operations  13.6 us (6%)
  other arithmetic  5.86 us (3%)
  starting transfers between devices  4.74 us (2%)
    psum x2, blocking collectives, per_device(): totals = lax.psum(partial_value, ('py', 'px'))  79.5 us
    all_to_all x1, waiting for transfers between devices, per_device(): lax.all_to_all(outgoing, 'px', split_axis=0, concat_axis=2, tiled=True)  43.9 us
    all_gather x1, waiting for transfers between devices, per_device(): span_all = lax.all_gather(traces, 'py', axis=0, tiled=True)  26.1 us
    dot_general x8, matrix products, per_device(): jnp.dot(current, gram[:, low:low + BLK], precision=lax.Precision.HIGHEST)  15.4 us
    all_gather x1, blocking collectives, per_device(): lax.all_gather(block_ids, 'px', axis=1, tiled=True).reshape(-1, SLOTS)  13.6 us
    dot_general x1, matrix products, accumulate(): lax.dot_general(tile_movie, picked, (((1,), (1,)), ((), ())), preferred_e...  5.2 us
    all_to_all x1, starting transfers between devices, per_device(): lax.all_to_all(outgoing, 'px', split_axis=0, concat_axis=2, tiled=True)  4.74 us
  transfers between devices with their start and end apart: 2, of which 2 were waited for; matrix products, arithmetic and copies ran while one was open for 2% of the time, Pallas kernels for 0%

commit v1 on v0

--- a/solution.py
+++ b/solution.py
@@ -28,7 +28,12 @@
     ids = block_ids.reshape(SLOTS)
     onehot = (ids[:, None] == jnp.arange(nblk, dtype=jnp.int32)[None, :]).astype(jnp.float32)
     live = jnp.sum(onehot, axis=1)
-    span_all = lax.all_gather(traces, "py", axis=0, tiled=True)
+    ring = [traces]
+    for hop in range(3):
+        ring.append(lax.ppermute(ring[-1], "py", [(dev, (dev + 1) % 4) for dev in range(4)]))
+    span_all = jnp.roll(
+        jnp.concatenate(ring[::-1], axis=0), (lax.axis_index("py") + 1) * ring[0].shape[0], axis=0
+    )
     span_len = span_all.shape[1]
     row_ids = lax.all_gather(block_ids, "px", axis=1, tiled=True).reshape(-1, SLOTS)
     route = (row_ids[:, :, None] == jnp.arange(nblk, dtype=jnp.int32)[None, None, :]).astype(

time: 234 us -> 222 us (0.949)
  between operations: 13.6 us -> 0.32 us
  starting transfers between devices: 4.74 us -> 8.34 us
    ppermute x0 -> x3, waiting for transfers between devices: none -> 27.5 us  [per_device(): lax.ppermute(ring[-1], 'py', [(dev, (dev + 1) % 4) for dev in range(4)])]
    all_gather x1 -> x0, waiting for transfers between devices: 26.1 us -> none  [per_device(): span_all = lax.all_gather(traces, 'py', axis=0, tiled=True)]
    ppermute x0 -> x3, starting transfers between devices: none -> 3.69 us  [per_device(): lax.ppermute(ring[-1], 'py', [(dev, (dev + 1) % 4) for dev in range(4)])]
  transfers between devices with their start and end apart: 2 -> 4, of which waited for: 2 -> 4; matrix products, arithmetic and copies ran while one was open for 2% -> 2% of each run, Pallas kernels for 0% -> 0%
where the time goes in v1:
time: 222 us; the launch traced here: 221 us
  blocking collectives  91.7 us (41%)
  waiting for transfers between devices  71.3 us (32%)
  matrix products  26.3 us (12%)
  local copies, waits for them, and re-layouts  17.4 us (8%)
  starting transfers between devices  8.34 us (4%)
  other arithmetic  5.86 us (3%)
    psum x2, blocking collectives, per_device(): totals = lax.psum(partial_value, ('py', 'px'))  79.8 us
    all_to_all x1, waiting for transfers between devices, per_device(): lax.all_to_all(outgoing, 'px', split_axis=0, concat_axis=2, tiled=True)  43.8 us
    ppermute x3, waiting for transfers between devices, per_device(): lax.ppermute(ring[-1], 'py', [(dev, (dev + 1) % 4) for dev in range(4)])  27.5 us
    dot_general x8, matrix products, per_device(): jnp.dot(current, gram[:, low:low + BLK], precision=lax.Precision.HIGHEST)  15.4 us
    all_gather x1, blocking collectives, per_device(): lax.all_gather(block_ids, 'px', axis=1, tiled=True).reshape(-1, SLOTS)  12 us
    dot_general x1, matrix products, accumulate(): lax.dot_general(tile_movie, picked, (((1,), (1,)), ((), ())), preferred_e...  5.2 us
    all_to_all x1, starting transfers between devices, per_device(): lax.all_to_all(outgoing, 'px', split_axis=0, concat_axis=2, tiled=True)  4.65 us
    gather x1, local copies, waits for them, and re-layouts, per_device(): denom = jnp.diagonal(gram) + 1e-06 + (1.0 - column_live)  4.52 us
  transfers between devices with their start and end apart: 4, of which 4 were waited for; matrix products, arithmetic and copies ran while one was open for 2% of the time, Pallas kernels for 0%

profile of v1, /device:TPU:0, one launch (start us, length us, event | category | flops | bytes accessed | tf_op | source)
XLA Modules:
  0.0 221.2 jit_solution(16169197345018727833)
XLA Ops:
  0.0 3.0 %collective-permute-start = (bf16[1024,256]{1,0:T(8,128)(2,1)}, bf16[1024,256]{1,0:T(8,128)(2,1)S(1)}, u32[]{:S(2)}, u32[]{:S(2)}) collective-permute-start(bf16[1024,256]{1,0:T(8,128)(2,1)} %param.21), channel_id=1, source_target_pairs={{0,8},{8,16},{16,24},{24,0},{1,9},{9,17},{17,25},{25,1},{2,10},{10... | collective-permute-start | bytes 1572872 | tf_op jit(solution)/shard_map/ppermute | solution.py:33
  3.0 13.2 %collective-permute-done = bf16[1024,256]{1,0:T(8,128)(2,1)S(1)} collective-permute-done((bf16[1024,256]{1,0:T(8,128)(2,1)}, bf16[1024,256]{1,0:T(8,128)(2,1)S(1)}, u32[]{:S(2)}, u32[]{:S(2)}) %collective-permute-start) | collective-permute-done | bytes 524320 | tf_op jit(solution)/shard_map/ppermute | solution.py:33
  16.8 13.3 %collective-permute-done.1 = bf16[1024,256]{1,0:T(8,128)(2,1)S(1)} collective-permute-done((bf16[1024,256]{1,0:T(8,128)(2,1)S(1)}, bf16[1024,256]{1,0:T(8,128)(2,1)S(1)}, u32[]{:S(2)}, u32[]{:S(2)}) %collective-permute-start.1) | collective-permute-done | bytes 524320 | tf_op jit(solution)/shard_map/ppermute | solution.py:33
  30.1 12.0 %all_gather.3 = s32[1,8,4]{2,0,1:T(1,128)S(1)} all-gather(s32[1,1,4]{2,0,1:T(1,128)} %bitcast.62), channel_id=1, replica_groups=mesh['py'=4,'px'=8] {'px'}, dimensions={1}, use_global_device_ids=true | all-gather | bytes 144 | tf_op jit(solution)/shard_map/all_gather | solution.py:38
  45.1 1.7 copy.50
  46.8 4.7 %all-to-all-start = ((bf16[8,512,256]{2,1,0:T(8,128)(2,1)}), bf16[8,512,256]{2,1,0:T(8,128)(2,1)}, u32[]{:S(2)}, u32[]{:S(2)}) async-start(bf16[8,512,256]{2,1,0:T(8,128)(2,1)} %copy.50), calls=%async_computation | async-start | bytes 4194304 | tf_op jit(solution)/shard_map/all_to_all | solution.py:49
  51.5 1.8 copy.46
  54.9 1.8 broadcast_multiply_fusion.2
  56.7 43.8 %all-to-all-done = bf16[8,512,256]{2,1,0:T(8,128)(2,1)} async-done(((bf16[8,512,256]{2,1,0:T(8,128)(2,1)}), bf16[8,512,256]{2,1,0:T(8,128)(2,1)}, u32[]{:S(2)}, u32[]{:S(2)}) %all-to-all-start) | async-done | bytes 2097184 | tf_op jit(solution)/shard_map/all_to_all | solution.py:49
  100.5 3.9 %copy.51 = bf16[1,512,8,256]{1,3,2,0:T(8,128)(2,1)} copy(bf16[1,512,8,256]{3,1,2,0:T(8,128)(2,1)} %bitcast.11) | data formatting | bytes 4194304 | tf_op jit(solution)/shard_map/all_to_all | solution.py:49
  104.4 3.5 %fusion.8 = f32[512,512]{1,0:T(8,128)S(1)} fusion(bf16[8,512,256]{2,1,0:T(8,128)(2,1)} %all-to-all-done), kind=kOutput, calls=%fused_computation.10 | convolution fusion | flops 1073741824 | bytes 3145728 | tf_op jit(solution)/shard_map/dot_general | solution.py:16
  107.9 4.5 %gather_fusion = f32[512]{0:T(512)S(1)} fusion(f32[512,512]{1,0:T(8,128)S(1)} %fusion.8, s32[512]{0:T(512)S(1)} %bitcast.56), kind=kCustom, calls=%fused_computation | custom fusion | bytes 8192 | tf_op jit(solution)/shard_map/jit(diagonal)/cond/branch_0_fun/gather | solution.py:53
  112.6 5.2 %convolution_bitcast_fusion = f32[1024,512]{0,1:T(8,128)S(1)} fusion(bf16[512,2048]{0,1:T(8,128)(2,1)} %bitcast.60, bf16[1024,2048]{1,0:T(8,128)(2,1)} %bitcast.68), kind=kOutput, calls=%fused_computation.9 | convolution fusion | flops 2147483648 | bytes 8388608 | tf_op jit(solution)/shard_map/dot_general | solution.py:13
  117.8 2.1 fusion.40
  119.9 2.1 fusion.36
  122.1 2.1 fusion.32
  124.2 1.5 fusion.28
  126.2 37.4 %psum.14 = f32[32,128]{1,0:T(8,128)S(1)} all-reduce(f32[32,128]{1,0:T(8,128)S(1)} %fusion.64), channel_id=1, replica_groups=mesh['py'=4,'px'=8] {'py','px'}, use_global_device_ids=true, to_apply=%region_5.6 | all-reduce | flops 4096 | bytes 32768 | tf_op jit(solution)/shard_map/psum | solution.py:68
  165.3 2.1 fusion.25
  167.4 2.1 fusion.21
  169.6 2.0 fusion.17
  175.0 42.4 %psum.15 = f32[32,128]{1,0:T(8,128)S(1)} all-reduce(f32[32,128]{1,0:T(8,128)S(1)} %fusion.62), channel_id=1, replica_groups=mesh['py'=4,'px'=8] {'py','px'}, use_global_device_ids=true, to_apply=%region_7.8 | all-reduce | flops 4096 | bytes 32768 | tf_op jit(solution)/shard_map/psum | solution.py:68
  217.6 1.8 broadcast_multiply_fusion
  219.4 1.8 copy.60
  (49 shorter events, 11.3 us)
Async XLA Ops:
  0.0 43.4 %copy-start.4 = (bf16[1024,256]{1,0:T(8,128)(2,1)S(1)}, bf16[1024,256]{1,0:T(8,128)(2,1)}, u32[]{:S(2)}) copy-start(bf16[1024,256]{1,0:T(8,128)(2,1)} %param.21) | copy-start | bytes 1572868
  0.0 16.1 %collective-permute-start = (bf16[1024,256]{1,0:T(8,128)(2,1)}, bf16[1024,256]{1,0:T(8,128)(2,1)S(1)}, u32[]{:S(2)}, u32[]{:S(2)}) collective-permute-start(bf16[1024,256]{1,0:T(8,128)(2,1)} %param.21), channel_id=1, source_target_pairs={{0,8},{8,16},{16,24},{24,0},{1,9},{9,17},{17,25},{25,1},{2,10},{10... | collective-permute-start | bytes 1572872 | tf_op jit(solution)/shard_map/ppermute | solution.py:33
  16.1 14.0 %collective-permute-start.1 = (bf16[1024,256]{1,0:T(8,128)(2,1)S(1)}, bf16[1024,256]{1,0:T(8,128)(2,1)S(1)}, u32[]{:S(2)}, u32[]{:S(2)}) collective-permute-start(bf16[1024,256]{1,0:T(8,128)(2,1)S(1)} %collective-permute-done), channel_id=1, source_target_pairs={{0,8},{8,16},{16,24},{24,0},{1,9},{9,17},{17,25},{25,1},{2,10},{10... | collective-permute-start | bytes 1572872 | tf_op jit(solution)/shard_map/ppermute | solution.py:33
  30.1 13.1 %collective-permute-start.2 = (bf16[1024,256]{1,0:T(8,128)(2,1)S(1)}, bf16[1024,256]{1,0:T(8,128)(2,1)S(1)}, u32[]{:S(2)}, u32[]{:S(2)}) collective-permute-start(bf16[1024,256]{1,0:T(8,128)(2,1)S(1)} %collective-permute-done.1), channel_id=1, source_target_pairs={{0,8},{8,16},{16,24},{24,0},{1,9},{9,17},{17,25},{25,1},{2,10},{10... | collective-permute-start | bytes 1572872 | tf_op jit(solution)/shard_map/ppermute | solution.py:33
  46.8 4.7 %copy-start.3 = (f32[64,16,512]{2,1,0:T(8,128)S(1)}, f32[64,16,512]{2,1,0:T(8,128)}, u32[]{:S(2)}) copy-start(f32[64,16,512]{2,1,0:T(8,128)} %param.22) | copy-start | bytes 6291460
  46.8 53.7 %all-to-all-start = ((bf16[8,512,256]{2,1,0:T(8,128)(2,1)}), bf16[8,512,256]{2,1,0:T(8,128)(2,1)}, u32[]{:S(2)}, u32[]{:S(2)}) async-start(bf16[8,512,256]{2,1,0:T(8,128)(2,1)} %copy.50), calls=%async_computation | async-start | bytes 4194304 | tf_op jit(solution)/shard_map/all_to_all | solution.py:49
  51.5 3.2 %copy-start.5 = (s32[1,1,4]{2,1,0:T(1,128)S(1)}, s32[1,1,4]{2,1,0:T(1,128)}, u32[]{:S(2)}) copy-start(s32[1,1,4]{2,1,0:T(1,128)} %param.23) | copy-start | bytes 52
  117.8 6.4 %copy-start.1 = (f32[1024,512]{0,1:T(8,128)}, f32[1024,512]{0,1:T(8,128)S(1)}, u32[]{:S(2)}) copy-start(f32[1024,512]{0,1:T(8,128)S(1)} %convolution_bitcast_fusion) | copy-start | bytes 6291460
  163.7 1.6 copy-start.2
  173.2 1.3 copy-start
